TPU v7x, 256 devices: a whole 4x4x8 slice. The times are simulated.
256 devices in a mesh: batch: 16 (over z, core), proto: 16 (over x, y).
Axes of the slice: x: 4, y: 4, z: 8, core: 2. Of those that a mesh axis runs over, the one named last changes fastest.
Arguments:
- slow_embed: bfloat16 [16384, 256], P('batch'), may hold values from -1 to 1
- fast_embed: bfloat16 [16384, 256], P('batch'), may hold values from -1 to 1
- prototypes: float32 [32768, 256], P('proto'), may hold values from -1 to 1
Outputs:
- proto_grad: float32 [32768, 256], P('proto')
- slow_grad: float32 [16384, 256], P('batch')
- fast_grad: float32 [16384, 256], P('batch')
All inputs are finite; a program needn't handle non-finite values.
Results may differ from a plain program's by a relative error of at most 0.0005.
The roundings to bfloat16 on the way count: a program that leaves them out, or rounds other values in their place, can miss the bound.
Values sent between devices are 32-bit elements; how exact they have to be, the bound alone decides.
A program may use at most 128 MiB of HBM per device.

v0:
```python
import jax
import jax.numpy as jnp
from jax import lax
from jax.sharding import PartitionSpec as P

ITERS = 3
CODE_EPS = 0.05
TEMPER = 0.1
NORM_EPS = 1e-06


def normalize(raw_rows):
    lengths = jnp.sqrt(jnp.sum(raw_rows * raw_rows, axis=-1, keepdims=True) + 1e-12)
    return (raw_rows / lengths, lengths)


def project_back(grad_unit, unit_vec, lengths):
    along = jnp.sum(unit_vec * grad_unit, axis=-1, keepdims=True)
    return (grad_unit - unit_vec * along) / lengths


def row_total(row_terms):
    return lax.psum(row_terms, "proto")


def normalizers(proto_square, embed_square, proto_entries, embed_entries):
    totals = lax.psum((proto_square, embed_square), ("batch", "proto"))
    proto_factor = lax.rsqrt(totals[0] / proto_entries + NORM_EPS)
    embed_factor = lax.rsqrt(totals[1] / embed_entries + NORM_EPS)
    return (proto_factor, embed_factor)


def body(slow_embed, fast_embed, prototypes):
    clip_dev = slow_embed.shape[0]
    proto_dev = prototypes.shape[0]
    feat_width = prototypes.shape[1]
    batch_count = lax.axis_size("batch")
    proto_count = lax.axis_size("proto")
    clips_all = clip_dev * batch_count
    protos_all = proto_dev * proto_count
    proto_entries = float(protos_all * feat_width)
    embed_entries = float(2 * clips_all * feat_width)
    raw_views = jnp.stack([slow_embed, fast_embed]).astype(jnp.float32)
    unit_vec, lengths = normalize(raw_views)
    unit_b = unit_vec.astype(jnp.bfloat16)
    proto_unit, proto_len = normalize(prototypes)
    proto_b = proto_unit.astype(jnp.bfloat16)
    scores = jnp.einsum("vbd,kd->vbk", unit_b, proto_b, preferred_element_type=jnp.float32)
    code_table = jnp.exp(scores / CODE_EPS)
    soft_exp = jnp.exp(scores / TEMPER)
    denom_terms = jnp.sum(soft_exp, axis=2)
    denominator = lax.psum(denom_terms, "proto")
    clip_scale = jnp.ones((2, clip_dev), jnp.float32)
    for iteration in range(ITERS):
        col_total = lax.psum(jnp.sum(code_table * clip_scale[:, :, None], axis=1), "batch")
        proto_scale = 1.0 / (protos_all * col_total)
        row_terms = jnp.sum(code_table * proto_scale[:, None, :], axis=2)
        if iteration == 0:
            clip_total = row_total(row_terms)
        else:
            clip_total = row_total(row_terms)
        clip_scale = 1.0 / (clips_all * clip_total)
    codes = code_table * proto_scale[:, None, :] / clip_total[:, :, None]
    probs = soft_exp / denominator[:, :, None]
    score_grad = (jnp.stack([probs[0] - codes[1], probs[1] - codes[0]]) / TEMPER).astype(
        jnp.bfloat16
    )
    proto_terms = jnp.einsum("vbk,vbd->kd", score_grad, unit_b, preferred_element_type=jnp.float32)
    grad_proto_unit = lax.psum(proto_terms, "batch")
    embed_terms = jnp.einsum("vbk,kd->vbd", score_grad, proto_b, preferred_element_type=jnp.float32)
    grad_unit = lax.psum(embed_terms, "proto")
    grad_proto = project_back(grad_proto_unit, proto_unit, proto_len)
    grad_embed = project_back(grad_unit, unit_vec, lengths)
    proto_factor, embed_factor = normalizers(
        jnp.sum(grad_proto * grad_proto) / batch_count,
        jnp.sum(grad_embed * grad_embed) / proto_count,
        proto_entries,
        embed_entries,
    )
    proto_grad = grad_proto * proto_factor
    slow_grad = grad_embed[0] * embed_factor
    fast_grad = grad_embed[1] * embed_factor
    return (proto_grad, slow_grad, fast_grad)


def solution(mesh):
    placed = (P("batch", None), P("batch", None), P("proto", None))
    return jax.shard_map(
        body,
        mesh=mesh,
        in_specs=placed,
        out_specs=(P("proto", None), P("batch", None), P("batch", None)),
        check_vma=False,
    )
```

profile of v0, /device:TPU:1, one launch (start us, length us, event | category | flops | bytes accessed | tf_op | source)
XLA Modules:
  0.0 716.6 jit_solution(129335976540485152)
XLA Ops:
  7.2 0.0 all-reduce.5.cloned.1.call-start
  7.2 1.6 fusion.5
  8.8 1.9 multiply_reduce_fusion.9
  10.7 9.2 %fusion.4 = (f32[2,2048]{1,0:T(2,128)S(1)}, f32[2,1024,2048]{2,1,0:T(8,128)}) fusion(f32[2048,256]{1,0:T(8,128)} %param.5, f32[2048]{0:T(1024)S(1)} %add_sqrt_fusion, f32[2,1024]{1,0:T(2,128)S(1)} %add_sqrt_fusion.1, bf16[1,1024,256]{2,1,0:T(8,128)(2,1)} %bitcast.16, bf16[1,1024,256]{2,1,0:T(8,128)(2,1)} %bitcast.20), kind=kOutput, calls=%fused_computation.15 | convolution fusion | flops 2159013888 | bytes 19955712 | tf_op jit(solution)/shard_map/vbd,kd->vbk/dot_general | solution.py:48
  20.0 48.8 %psum.78 = f32[2,2048]{1,0:T(2,128)S(1)} all-reduce(f32[2,2048]{1,0:T(2,128)S(1)} %get-tuple-element.17), channel_id=1, replica_groups=mesh['batch'=16,'proto'=16] {'batch'}, use_global_device_ids=true, to_apply=%region_5.0 | all-reduce | flops 4096 | bytes 32768 | tf_op jit(solution)/shard_map/psum | solution.py:55
  68.8 9.0 %fusion.3 = (f32[2,1024]{1,0:T(2,128)S(1)}, f32[2,1024]{1,0:T(2,128)S(1)}) fusion(f32[2,1024,2048]{2,1,0:T(8,128)} %get-tuple-element.18, f32[2,2048]{1,0:T(2,128)S(1)} %multiply_divide_fusion.3), kind=kLoop, calls=%fused_computation.12 | loop fusion | flops 20967424 | bytes 16809984 | tf_op jit(solution)/shard_map/reduce_sum | solution.py:51
  77.8 34.0 %psum.79 = f32[2,1024]{1,0:T(2,128)S(1)} all-reduce(f32[2,1024]{1,0:T(2,128)S(1)} %get-tuple-element.4), channel_id=1, replica_groups=mesh['batch'=16,'proto'=16] {'proto'}, use_global_device_ids=true, to_apply=%region_7.0 | all-reduce | flops 2048 | bytes 16384 | tf_op jit(solution)/shard_map/psum | solution.py:23
  111.8 7.4 %multiply_reduce_fusion.2 = f32[2,2048]{1,0:T(2,128)S(1)} fusion(f32[2,1024]{1,0:T(2,128)S(1)} %multiply_divide_fusion.5, f32[2,1024,2048]{2,1,0:T(8,128)} %get-tuple-element.18), kind=kLoop, calls=%fused_computation.5 | loop fusion | flops 12578816 | bytes 16801792 | tf_op jit(solution)/shard_map/reduce_sum | solution.py:55
  119.1 52.9 %psum.80 = f32[2,2048]{1,0:T(2,128)S(1)} all-reduce(f32[2,2048]{1,0:T(2,128)S(1)} %multiply_reduce_fusion.2), channel_id=1, replica_groups=mesh['batch'=16,'proto'=16] {'batch'}, use_global_device_ids=true, to_apply=%region_9.0 | all-reduce | flops 4096 | bytes 32768 | tf_op jit(solution)/shard_map/psum | solution.py:55
  172.0 8.6 %multiply_reduce_fusion.1 = f32[2,1024]{1,0:T(2,128)S(1)} fusion(f32[2,2048]{1,0:T(2,128)S(1)} %multiply_divide_fusion.2, f32[2,1024,2048]{2,1,0:T(8,128)} %get-tuple-element.18), kind=kLoop, calls=%fused_computation.4 | loop fusion | flops 12580864 | bytes 16801792 | tf_op jit(solution)/shard_map/reduce_sum | solution.py:57
  180.6 29.0 %psum.81 = f32[2,1024]{1,0:T(2,128)S(1)} all-reduce(f32[2,1024]{1,0:T(2,128)S(1)} %multiply_reduce_fusion.1), channel_id=1, replica_groups=mesh['batch'=16,'proto'=16] {'proto'}, use_global_device_ids=true, to_apply=%region_11.0 | all-reduce | flops 2048 | bytes 16384 | tf_op jit(solution)/shard_map/psum | solution.py:23
  209.7 7.4 %multiply_reduce_fusion = f32[2,2048]{1,0:T(2,128)S(1)} fusion(f32[2,1024]{1,0:T(2,128)S(1)} %multiply_divide_fusion.4, f32[2,1024,2048]{2,1,0:T(8,128)} %get-tuple-element.18), kind=kLoop, calls=%fused_computation.3 | loop fusion | flops 12578816 | bytes 16801792 | tf_op jit(solution)/shard_map/reduce_sum | solution.py:55
  217.0 52.8 %psum.82 = f32[2,2048]{1,0:T(2,128)S(1)} all-reduce(f32[2,2048]{1,0:T(2,128)S(1)} %multiply_reduce_fusion), channel_id=1, replica_groups=mesh['batch'=16,'proto'=16] {'batch'}, use_global_device_ids=true, to_apply=%region_13.0 | all-reduce | flops 4096 | bytes 32768 | tf_op jit(solution)/shard_map/psum | solution.py:55
  269.9 8.6 %multiply_reduce_fusion.4 = f32[2,1024]{1,0:T(2,128)S(1)} fusion(f32[2,2048]{1,0:T(2,128)S(1)} %multiply_divide_fusion.1, f32[2,1024,2048]{2,1,0:T(8,128)} %get-tuple-element.18), kind=kLoop, calls=%fused_computation.10 | loop fusion | flops 12580864 | bytes 16801792 | tf_op jit(solution)/shard_map/reduce_sum | solution.py:57
  278.5 57.5 %all-reduce.1 = (f32[2,1024]{1,0:T(2,128)S(1)}, f32[2,1024]{1,0:T(2,128)S(1)}) all-reduce(f32[2,1024]{1,0:T(2,128)S(1)} %multiply_reduce_fusion.4, f32[2,1024]{1,0:T(2,128)S(1)} %get-tuple-element.3), channel_id=1, replica_groups=mesh['batch'=16,'proto'=16] {'proto'}, use_global_device_ids=true, to_apply=%region_15.0 | all-reduce | flops 4096 | bytes 32768 | tf_op jit(solution)/shard_map/psum | solution.py:23
  336.0 18.3 %fusion.2 = (f32[2,1024,2048]{2,1,0:T(8,128)}, f32[2,1024,2048]{2,1,0:T(8,128)}) fusion(f32[2,1024,2048]{2,1,0:T(8,128)} %get-tuple-element.18, f32[2,1024]{1,0:T(2,128)S(1)} %get-tuple-element.8, f32[2,1024]{1,0:T(2,128)S(1)} %get-tuple-element.7, f32[2,2048]{1,0:T(2,128)S(1)} %multiply_divide_fusion.1), kind=kLoop, calls=%fused_computation.11 | loop fusion | flops 20971520 | bytes 50364416 | tf_op jit(solution)/shard_map/div | solution.py:64
  354.3 19.2 %slice_subtract_fusion.1 = (f32[1,1024,2048]{2,1,0:T(8,128)}, f32[1,1024,2048]{2,1,0:T(8,128)}) fusion(f32[2,1024,2048]{2,1,0:T(8,128)} %get-tuple-element.14, f32[2,1024,2048]{2,1,0:T(8,128)} %get-tuple-element.13), kind=kLoop, calls=%fused_computation.14 | loop fusion | flops 4194304 | bytes 50331648 | tf_op jit(solution)/shard_map/sub | solution.py:65
  373.5 0.0 copy-start
  373.5 8.8 %convolution_bitcast_fusion = f32[2048,256]{1,0:T(8,128)} fusion(f32[1,1024,2048]{2,1,0:T(8,128)} %get-tuple-element.12, f32[1,1024,2048]{2,1,0:T(8,128)} %get-tuple-element.11, f32[2,1024]{1,0:T(2,128)S(1)} %add_sqrt_fusion.1, bf16[1,1024,256]{2,1,0:T(8,128)(2,1)S(1)} %bitcast.17, bf16[1,1024,256]{2,1,0:T(8,128)(2,1)S(1)} %bitcast.21), kind=kOutput, calls=%fused_computation.16 | convolution fusion | flops 2162163712 | bytes 19931136 | tf_op jit(solution)/shard_map/vbk,vbd->kd/dot_general | solution.py:68
  382.3 0.0 all-reduce.5.cloned.1.call-update
  382.3 0.3 all-reduce.7.cloned.1.call-start
  382.6 8.5 %fusion.11 = f32[2,1024,256]{2,1,0:T(8,128)} fusion(f32[1,1024,2048]{2,1,0:T(8,128)} %get-tuple-element.12, f32[1,1024,2048]{2,1,0:T(8,128)} %get-tuple-element.11, f32[2048,256]{1,0:T(8,128)S(1)} %copy-done, f32[2048]{0:T(1024)S(1)} %add_sqrt_fusion), kind=kOutput, calls=%fused_computation.33 | convolution fusion | flops 2161115136 | bytes 20979712 | tf_op jit(solution)/shard_map/vbk,kd->vbd/dot_general | solution.py:70
  391.1 0.0 all-reduce.7.cloned.1.call-update
  391.2 116.1 %all-reduce.5.cloned.1.call-done = f32[2048,256]{1,0:T(8,128)} async-done(((f32[2048,256]{1,0:T(8,128)}), f32[2048,256]{1,0:T(8,128)}) %all-reduce.5.cloned.1.call-update) | async-done | bytes 2097168 | tf_op jit(solution)/shard_map/psum | solution.py:69
  507.3 2.2 multiply_reduce_fusion.8
  509.5 3.6 multiply_reduce_fusion.7
  513.8 0.0 copy-start.1
  513.8 97.2 %all-reduce.7.cloned.1.call-done = f32[2,1024,256]{2,1,0:T(8,128)} async-done(((f32[2,1024,256]{2,1,0:T(8,128)}), f32[2,1024,256]{2,1,0:T(8,128)}) %all-reduce.7.cloned.1.call-update) | async-done | bytes 2097168 | tf_op jit(solution)/shard_map/psum | solution.py:71
  611.0 15.5 %multiply_reduce_fusion.5 = (f32[]{:T(128)}, f32[2,1024,256]{2,1,0:T(8,128)}) fusion(f32[2,1024,256]{2,1,0:T(8,128)} %all-reduce.7.cloned.1.call-done, f32[2,1024]{1,0:T(2,128)S(1)} %add_sqrt_fusion.1, bf16[1,1024,256]{2,1,0:T(8,128)(2,1)S(1)} %bitcast.18, bf16[1,1024,256]{2,1,0:T(8,128)(2,1)S(1)} %bitcast.22), kind=kOutput, calls=%fused_computation.20 | output fusion | flops 7342334 | bytes 5251076 | tf_op jit(solution)/shard_map/mul | solution.py:19
  627.1 76.8 %all-reduce = (f32[]{:T(128)}, f32[]{:T(128)}) all-reduce(f32[]{:T(128)S(6)} %div.101, f32[]{:T(128)S(6)} %div.104), channel_id=1, replica_groups=mesh['batch'=16,'proto'=16] {'batch','proto'}, use_global_device_ids=true, to_apply=%region_19.0 | all-reduce | flops 2 | bytes 16 | tf_op jit(solution)/shard_map/psum | solution.py:27
  705.3 1.5 broadcast_multiply_fusion
  706.8 3.0 fusion.9
  (13 shorter events, 0.1 us)
Async XLA Ops:
  7.2 500.1 %all-reduce.5.cloned.1.call-start = ((), (), s32[]{:S(2)}) async-start(), calls=%async_computation | async-start | bytes 4194304 | tf_op jit(solution)/shard_map/psum | solution.py:69
  354.3 19.2 %copy-start.2 = (bf16[1024,256]{1,0:T(8,128)(2,1)S(1)}, bf16[1024,256]{1,0:T(8,128)(2,1)}, u32[]{:S(2)}) copy-start(bf16[1024,256]{1,0:T(8,128)(2,1)} %param.4) | copy-start | bytes 1572868
  354.3 19.2 %copy-start.3 = (bf16[1024,256]{1,0:T(8,128)(2,1)S(1)}, bf16[1024,256]{1,0:T(8,128)(2,1)}, u32[]{:S(2)}) copy-start(bf16[1024,256]{1,0:T(8,128)(2,1)} %param.3) | copy-start | bytes 1572868
  373.5 9.1 %copy-start = (f32[2048,256]{1,0:T(8,128)S(1)}, f32[2048,256]{1,0:T(8,128)}, u32[]{:S(2)}) copy-start(f32[2048,256]{1,0:T(8,128)} %param.5) | copy-start | bytes 6291460
  382.3 228.7 %all-reduce.7.cloned.1.call-start = ((), (), s32[]{:S(2)}) async-start(), calls=%async_computation.1 | async-start | bytes 4194304 | tf_op jit(solution)/shard_map/psum | solution.py:71
  513.8 191.5 %copy-start.1 = (f32[2048,256]{1,0:T(8,128)S(1)}, f32[2048,256]{1,0:T(8,128)}, u32[]{:S(2)}) copy-start(f32[2048,256]{1,0:T(8,128)} %get-tuple-element.10) | copy-start | bytes 6291460
Sparse Core Ops, SparseCore 0:
  382.4 124.8 all-reduce.4
  510.6 100.3 all-reduce.6
where the time goes:
time: 717 us
  blocking collectives  352 us (49%)
  waiting for transfers between devices  213 us (30%)
  other arithmetic  108 us (15%)
  matrix products  26.5 us (4%)
  between operations  16.9 us (2%)
    psum x3, blocking collectives, body(): lax.psum(jnp.sum(code_table * clip_scale[:, :, None], axis=1), 'batch')  155 us
    psum x3, blocking collectives, row_total(): return lax.psum(row_terms, 'proto')  121 us
    psum x1, waiting for transfers between devices, body(): grad_proto_unit = lax.psum(proto_terms, 'batch')  116 us
    psum x1, waiting for transfers between devices, body(): grad_unit = lax.psum(embed_terms, 'proto')  97.2 us
    psum x1, blocking collectives, normalizers(): totals = lax.psum((proto_square, embed_square), ('batch', 'proto'))  76.8 us
    sub x1, other arithmetic, body(): probs[0] - codes[1]  19.2 us
    div x1, other arithmetic, body(): probs = soft_exp / denominator[:, :, None]  18.3 us
    reduce_sum x2, other arithmetic, body(): row_terms = jnp.sum(code_table * proto_scale[:, None, :], axis=2)  17.2 us
  transfers between devices with their start and end apart: 2, of which 2 were waited for; matrix products, arithmetic and copies ran while one was open for 2% of the time, Pallas kernels for 0%

commit v1 on v0

--- a/solution.py
+++ b/solution.py
@@ -24,7 +24,7 @@
 
 
 def normalizers(proto_square, embed_square, proto_entries, embed_entries):
-    totals = lax.psum((proto_square, embed_square), ("batch", "proto"))
+    totals = lax.psum(lax.psum((proto_square, embed_square), "batch"), "proto")
     proto_factor = lax.rsqrt(totals[0] / proto_entries + NORM_EPS)
     embed_factor = lax.rsqrt(totals[1] / embed_entries + NORM_EPS)
     return (proto_factor, embed_factor)

time: 717 us -> 704 us (0.982)
  blocking collectives: 352 us -> 332 us
    psum x1 -> x2, blocking collectives: 76.8 us -> 57.4 us  [normalizers(): totals = lax.psum(lax.psum((proto_square, embed_square), 'batch'), 'proto')]
where the time goes in v1:
time: 704 us; the launch traced here: 697 us
  blocking collectives  332 us (47%)
  waiting for transfers between devices  213 us (30%)
  other arithmetic  108 us (15%)
  matrix products  26.5 us (4%)
  between operations  16.9 us (2%)
    psum x3, blocking collectives, body(): lax.psum(jnp.sum(code_table * clip_scale[:, :, None], axis=1), 'batch')  155 us
    psum x3, blocking collectives, row_total(): return lax.psum(row_terms, 'proto')  121 us
    psum x1, waiting for transfers between devices, body(): grad_proto_unit = lax.psum(proto_terms, 'batch')  116 us
    psum x1, waiting for transfers between devices, body(): grad_unit = lax.psum(embed_terms, 'proto')  97.2 us
    psum x2, blocking collectives, normalizers(): totals = lax.psum(lax.psum((proto_square, embed_square), 'batch'), 'proto')  57.4 us
    sub x1, other arithmetic, body(): probs[0] - codes[1]  19.2 us
    div x1, other arithmetic, body(): probs = soft_exp / denominator[:, :, None]  18.3 us
    reduce_sum x2, other arithmetic, body(): row_terms = jnp.sum(code_table * proto_scale[:, None, :], axis=2)  17.2 us
  transfers between devices with their start and end apart: 2, of which 2 were waited for; matrix products, arithmetic and copies ran while one was open for 2% of the time, Pallas kernels for 0%

profile of v1, /device:TPU:1, one launch (start us, length us, event | category | flops | bytes accessed | tf_op | source)
XLA Modules:
  0.0 697.2 jit_solution(8995747704545140042)
XLA Ops:
  7.2 0.0 all-reduce.6.cloned.1.call-start
  7.2 1.6 fusion.5
  8.8 1.9 multiply_reduce_fusion.9
  10.7 9.2 %fusion.4 = (f32[2,2048]{1,0:T(2,128)S(1)}, f32[2,1024,2048]{2,1,0:T(8,128)}) fusion(f32[2048,256]{1,0:T(8,128)} %param.5, f32[2048]{0:T(1024)S(1)} %add_sqrt_fusion, f32[2,1024]{1,0:T(2,128)S(1)} %add_sqrt_fusion.1, bf16[1,1024,256]{2,1,0:T(8,128)(2,1)} %bitcast.16, bf16[1,1024,256]{2,1,0:T(8,128)(2,1)} %bitcast.20), kind=kOutput, calls=%fused_computation.15 | convolution fusion | flops 2159013888 | bytes 19955712 | tf_op jit(solution)/shard_map/vbd,kd->vbk/dot_general | solution.py:48
  20.0 48.8 %psum.92 = f32[2,2048]{1,0:T(2,128)S(1)} all-reduce(f32[2,2048]{1,0:T(2,128)S(1)} %get-tuple-element.19), channel_id=1, replica_groups=mesh['batch'=16,'proto'=16] {'batch'}, use_global_device_ids=true, to_apply=%region_5.0 | all-reduce | flops 4096 | bytes 32768 | tf_op jit(solution)/shard_map/psum | solution.py:55
  68.8 9.0 %fusion.3 = (f32[2,1024]{1,0:T(2,128)S(1)}, f32[2,1024]{1,0:T(2,128)S(1)}) fusion(f32[2,1024,2048]{2,1,0:T(8,128)} %get-tuple-element.20, f32[2,2048]{1,0:T(2,128)S(1)} %multiply_divide_fusion.3), kind=kLoop, calls=%fused_computation.12 | loop fusion | flops 20967424 | bytes 16809984 | tf_op jit(solution)/shard_map/reduce_sum | solution.py:51
  77.8 34.0 %psum.93 = f32[2,1024]{1,0:T(2,128)S(1)} all-reduce(f32[2,1024]{1,0:T(2,128)S(1)} %get-tuple-element.4), channel_id=1, replica_groups=mesh['batch'=16,'proto'=16] {'proto'}, use_global_device_ids=true, to_apply=%region_7.0 | all-reduce | flops 2048 | bytes 16384 | tf_op jit(solution)/shard_map/psum | solution.py:23
  111.8 7.4 %multiply_reduce_fusion.2 = f32[2,2048]{1,0:T(2,128)S(1)} fusion(f32[2,1024]{1,0:T(2,128)S(1)} %multiply_divide_fusion.5, f32[2,1024,2048]{2,1,0:T(8,128)} %get-tuple-element.20), kind=kLoop, calls=%fused_computation.5 | loop fusion | flops 12578816 | bytes 16801792 | tf_op jit(solution)/shard_map/reduce_sum | solution.py:55
  119.1 52.9 %psum.94 = f32[2,2048]{1,0:T(2,128)S(1)} all-reduce(f32[2,2048]{1,0:T(2,128)S(1)} %multiply_reduce_fusion.2), channel_id=1, replica_groups=mesh['batch'=16,'proto'=16] {'batch'}, use_global_device_ids=true, to_apply=%region_9.0 | all-reduce | flops 4096 | bytes 32768 | tf_op jit(solution)/shard_map/psum | solution.py:55
  172.0 8.6 %multiply_reduce_fusion.1 = f32[2,1024]{1,0:T(2,128)S(1)} fusion(f32[2,2048]{1,0:T(2,128)S(1)} %multiply_divide_fusion.2, f32[2,1024,2048]{2,1,0:T(8,128)} %get-tuple-element.20), kind=kLoop, calls=%fused_computation.4 | loop fusion | flops 12580864 | bytes 16801792 | tf_op jit(solution)/shard_map/reduce_sum | solution.py:57
  180.6 29.0 %psum.95 = f32[2,1024]{1,0:T(2,128)S(1)} all-reduce(f32[2,1024]{1,0:T(2,128)S(1)} %multiply_reduce_fusion.1), channel_id=1, replica_groups=mesh['batch'=16,'proto'=16] {'proto'}, use_global_device_ids=true, to_apply=%region_11.0 | all-reduce | flops 2048 | bytes 16384 | tf_op jit(solution)/shard_map/psum | solution.py:23
  209.7 7.4 %multiply_reduce_fusion = f32[2,2048]{1,0:T(2,128)S(1)} fusion(f32[2,1024]{1,0:T(2,128)S(1)} %multiply_divide_fusion.4, f32[2,1024,2048]{2,1,0:T(8,128)} %get-tuple-element.20), kind=kLoop, calls=%fused_computation.3 | loop fusion | flops 12578816 | bytes 16801792 | tf_op jit(solution)/shard_map/reduce_sum | solution.py:55
  217.0 52.8 %psum.96 = f32[2,2048]{1,0:T(2,128)S(1)} all-reduce(f32[2,2048]{1,0:T(2,128)S(1)} %multiply_reduce_fusion), channel_id=1, replica_groups=mesh['batch'=16,'proto'=16] {'batch'}, use_global_device_ids=true, to_apply=%region_13.0 | all-reduce | flops 4096 | bytes 32768 | tf_op jit(solution)/shard_map/psum | solution.py:55
  269.9 8.6 %multiply_reduce_fusion.4 = f32[2,1024]{1,0:T(2,128)S(1)} fusion(f32[2,2048]{1,0:T(2,128)S(1)} %multiply_divide_fusion.1, f32[2,1024,2048]{2,1,0:T(8,128)} %get-tuple-element.20), kind=kLoop, calls=%fused_computation.10 | loop fusion | flops 12580864 | bytes 16801792 | tf_op jit(solution)/shard_map/reduce_sum | solution.py:57
  278.5 57.5 %all-reduce.1 = (f32[2,1024]{1,0:T(2,128)S(1)}, f32[2,1024]{1,0:T(2,128)S(1)}) all-reduce(f32[2,1024]{1,0:T(2,128)S(1)} %multiply_reduce_fusion.4, f32[2,1024]{1,0:T(2,128)S(1)} %get-tuple-element.3), channel_id=1, replica_groups=mesh['batch'=16,'proto'=16] {'proto'}, use_global_device_ids=true, to_apply=%region_15.0 | all-reduce | flops 4096 | bytes 32768 | tf_op jit(solution)/shard_map/psum | solution.py:23
  336.0 18.3 %fusion.2 = (f32[2,1024,2048]{2,1,0:T(8,128)}, f32[2,1024,2048]{2,1,0:T(8,128)}) fusion(f32[2,1024,2048]{2,1,0:T(8,128)} %get-tuple-element.20, f32[2,1024]{1,0:T(2,128)S(1)} %get-tuple-element.8, f32[2,1024]{1,0:T(2,128)S(1)} %get-tuple-element.7, f32[2,2048]{1,0:T(2,128)S(1)} %multiply_divide_fusion.1), kind=kLoop, calls=%fused_computation.11 | loop fusion | flops 20971520 | bytes 50364416 | tf_op jit(solution)/shard_map/div | solution.py:64
  354.3 19.2 %slice_subtract_fusion.1 = (f32[1,1024,2048]{2,1,0:T(8,128)}, f32[1,1024,2048]{2,1,0:T(8,128)}) fusion(f32[2,1024,2048]{2,1,0:T(8,128)} %get-tuple-element.16, f32[2,1024,2048]{2,1,0:T(8,128)} %get-tuple-element.15), kind=kLoop, calls=%fused_computation.14 | loop fusion | flops 4194304 | bytes 50331648 | tf_op jit(solution)/shard_map/sub | solution.py:65
  373.5 0.0 copy-start
  373.5 8.8 %convolution_bitcast_fusion = f32[2048,256]{1,0:T(8,128)} fusion(f32[1,1024,2048]{2,1,0:T(8,128)} %get-tuple-element.14, f32[1,1024,2048]{2,1,0:T(8,128)} %get-tuple-element.13, f32[2,1024]{1,0:T(2,128)S(1)} %add_sqrt_fusion.1, bf16[1,1024,256]{2,1,0:T(8,128)(2,1)S(1)} %bitcast.17, bf16[1,1024,256]{2,1,0:T(8,128)(2,1)S(1)} %bitcast.21), kind=kOutput, calls=%fused_computation.16 | convolution fusion | flops 2162163712 | bytes 19931136 | tf_op jit(solution)/shard_map/vbk,vbd->kd/dot_general | solution.py:68
  382.3 0.0 all-reduce.6.cloned.1.call-update
  382.3 0.3 all-reduce.8.cloned.1.call-start
  382.6 8.5 %fusion.11 = f32[2,1024,256]{2,1,0:T(8,128)} fusion(f32[1,1024,2048]{2,1,0:T(8,128)} %get-tuple-element.14, f32[1,1024,2048]{2,1,0:T(8,128)} %get-tuple-element.13, f32[2048,256]{1,0:T(8,128)S(1)} %copy-done, f32[2048]{0:T(1024)S(1)} %add_sqrt_fusion), kind=kOutput, calls=%fused_computation.33 | convolution fusion | flops 2161115136 | bytes 20979712 | tf_op jit(solution)/shard_map/vbk,kd->vbd/dot_general | solution.py:70
  391.1 0.0 all-reduce.8.cloned.1.call-update
  391.2 116.1 %all-reduce.6.cloned.1.call-done = f32[2048,256]{1,0:T(8,128)} async-done(((f32[2048,256]{1,0:T(8,128)}), f32[2048,256]{1,0:T(8,128)}) %all-reduce.6.cloned.1.call-update) | async-done | bytes 2097168 | tf_op jit(solution)/shard_map/psum | solution.py:69
  507.3 2.2 multiply_reduce_fusion.8
  509.5 3.6 multiply_reduce_fusion.7
  513.8 97.2 %all-reduce.8.cloned.1.call-done = f32[2,1024,256]{2,1,0:T(8,128)} async-done(((f32[2,1024,256]{2,1,0:T(8,128)}), f32[2,1024,256]{2,1,0:T(8,128)}) %all-reduce.8.cloned.1.call-update) | async-done | bytes 2097168 | tf_op jit(solution)/shard_map/psum | solution.py:71
  611.0 15.5 %multiply_reduce_fusion.5 = (f32[]{:T(128)}, f32[2,1024,256]{2,1,0:T(8,128)}) fusion(f32[2,1024,256]{2,1,0:T(8,128)} %all-reduce.8.cloned.1.call-done, f32[2,1024]{1,0:T(2,128)S(1)} %add_sqrt_fusion.1, bf16[1,1024,256]{2,1,0:T(8,128)(2,1)S(1)} %bitcast.18, bf16[1,1024,256]{2,1,0:T(8,128)(2,1)S(1)} %bitcast.22), kind=kOutput, calls=%fused_computation.20 | output fusion | flops 7342334 | bytes 5251076 | tf_op jit(solution)/shard_map/mul | solution.py:19
  627.1 25.9 %all-reduce.2 = (f32[]{:T(128)}, f32[]{:T(128)}) all-reduce(f32[]{:T(128)S(6)} %div.101, f32[]{:T(128)S(6)} %div.104), channel_id=1, replica_groups=mesh['batch'=16,'proto'=16] {'batch'}, use_global_device_ids=true, to_apply=%region_19.0 | all-reduce | flops 2 | bytes 16 | tf_op jit(solution)/shard_map/psum | solution.py:27
  653.0 31.5 %all-reduce = (f32[]{:T(128)}, f32[]{:T(128)}) all-reduce(f32[]{:T(128)} %get-tuple-element.9, f32[]{:T(128)} %get-tuple-element.10), channel_id=1, replica_groups=mesh['batch'=16,'proto'=16] {'proto'}, use_global_device_ids=true, to_apply=%region_20.0 | all-reduce | flops 2 | bytes 16 | tf_op jit(solution)/shard_map/psum | solution.py:27
  685.9 1.5 broadcast_multiply_fusion
  687.4 3.0 fusion.9
  (14 shorter events, 0.1 us)
Async XLA Ops:
  7.2 500.1 %all-reduce.6.cloned.1.call-start = ((), (), s32[]{:S(2)}) async-start(), calls=%async_computation | async-start | bytes 4194304 | tf_op jit(solution)/shard_map/psum | solution.py:69
  354.3 19.2 %copy-start.2 = (bf16[1024,256]{1,0:T(8,128)(2,1)S(1)}, bf16[1024,256]{1,0:T(8,128)(2,1)}, u32[]{:S(2)}) copy-start(bf16[1024,256]{1,0:T(8,128)(2,1)} %param.4) | copy-start | bytes 1572868
  354.3 19.2 %copy-start.3 = (bf16[1024,256]{1,0:T(8,128)(2,1)S(1)}, bf16[1024,256]{1,0:T(8,128)(2,1)}, u32[]{:S(2)}) copy-start(bf16[1024,256]{1,0:T(8,128)(2,1)} %param.3) | copy-start | bytes 1572868
  373.5 9.1 %copy-start = (f32[2048,256]{1,0:T(8,128)S(1)}, f32[2048,256]{1,0:T(8,128)}, u32[]{:S(2)}) copy-start(f32[2048,256]{1,0:T(8,128)} %param.5) | copy-start | bytes 6291460
  382.3 228.7 %all-reduce.8.cloned.1.call-start = ((), (), s32[]{:S(2)}) async-start(), calls=%async_computation.1 | async-start | bytes 4194304 | tf_op jit(solution)/shard_map/psum | solution.py:71
  513.8 172.1 %copy-start.1 = (f32[2048,256]{1,0:T(8,128)S(1)}, f32[2048,256]{1,0:T(8,128)}, u32[]{:S(2)}) copy-start(f32[2048,256]{1,0:T(8,128)} %get-tuple-element.12) | copy-start | bytes 6291460
Sparse Core Ops, SparseCore 0:
  382.4 124.8 all-reduce.5
  510.6 100.3 all-reduce.7
